TPU v7x, 32 devices: a whole 2x2x4 slice. The times are simulated.
32 devices in a mesh: grp: 2 (over y), row: 4 (over x, core), col: 4 (over z).
Axes of the slice: x: 2, y: 2, z: 4, core: 2. Of those that a mesh axis runs over, the one named last changes fastest.
Arguments:
- dosage: float32 [16384, 2048], P(('grp', 'row'), 'col'), parts along dimension 0, as said below
- phenotypes: float32 [16384, 64], P(('grp', 'row'), 'col'), parts along dimension 0, may hold values from -6 to 6
- solution: float32 [4096, 64], P(('grp', 'col')), parts along dimension 0, may hold values from -6 to 6
- inverse_factor: float32 [4096, 2048], P(('grp', 'col'), 'row'), parts along dimension 0, as said below
Outputs:
- residual: float32 [16384, 64], P(('grp', 'row'), 'col'), parts along dimension 0
- correction: float32 [4096, 64], P(('grp', 'col')), parts along dimension 0
There are 2 independent parts, one for each index of `grp`. A program takes and returns all parts, laid end to end along the dimension named above; each array names one. Nothing has to cross between parts.
Inputs may be any that keep to these rules, and one draw needn't show every extreme that they name: `dosage`: dense real-valued entries. `inverse_factor`: upper triangular: entries below the diagonal are zero, diagonal entries positive; a given preconditioner, not derived from the slab's values.
All inputs are finite; a program needn't handle non-finite values.
Results may differ from a plain program's by a relative error of at most 0.00013.
Values sent between devices are 32-bit elements; how exact they have to be, the bound alone decides.
A program may use at most 64 MiB of HBM per device.

v0:
```python
import jax
import jax.numpy as jnp
from jax import lax
from jax.sharding import PartitionSpec as P

ITERS = 2


def transposed_product(left, right):
    return lax.dot_general(
        left,
        right,
        (((0,), (0,)), ((), ())),
        precision=lax.Precision.HIGHEST,
        preferred_element_type=jnp.float32,
    )


def plain_product(left, right):
    return jnp.dot(left, right, precision=lax.Precision.HIGHEST, preferred_element_type=jnp.float32)


def local(dosage, phenotypes, solution, inverse_factor):

    def residual_parts(field):
        fitted = plain_product(dosage, field)
        own = phenotypes - lax.psum_scatter(fitted, "col", scatter_dimension=1, tiled=True)
        return (own, own)

    field = solution
    total = jnp.zeros_like(solution)
    for step in range(ITERS):
        own, whole = residual_parts(field)
        partial_value = transposed_product(dosage, lax.all_gather(own, "col", axis=1, tiled=True))
        inner = lax.psum(transposed_product(inverse_factor, lax.psum(partial_value, "row")), "col")
        change = lax.psum(plain_product(inverse_factor, inner), "row")
        field = field + change
        total = total + change
    own, whole = residual_parts(field)
    return (own, total)


def solution(mesh):
    return jax.shard_map(
        local,
        mesh=mesh,
        in_specs=(
            P(("grp", "row"), "col"),
            P(("grp", "row"), "col"),
            P(("grp", "col"), None),
            P(("grp", "col"), "row"),
        ),
        out_specs=(P(("grp", "row"), "col"), P(("grp", "col"), None)),
        check_vma=False,
    )
```

profile of v0, /device:TPU:0, one launch (start us, length us, event | category | flops | bytes accessed | tf_op | source)
XLA Modules:
  0.0 355.0 jit_solution(17227823966330348009)
XLA Ops:
  7.2 7.2 %fusion.1 = f32[2048,64]{0,1:T(8,128)} fusion(f32[2048,512]{1,0:T(8,128)} %param.4, f32[512,64]{0,1:T(8,128)} %param.6), kind=kOutput, calls=%fused_computation.9 | convolution fusion | flops 805306368 | bytes 4849664 | tf_op jit(solution)/shard_map/dot_general | solution.py:20
  14.5 24.7 %reduce-scatter.4.cloned.1.call-done = f32[2048,16]{0,1:T(8,128)} async-done(((f32[2048,64]{0,1:T(8,128)}), f32[2048,16]{0,1:T(8,128)}) %reduce-scatter.4.cloned.1.call-update) | async-done | bytes 131088 | tf_op jit(solution)/shard_map/reduce_scatter | solution.py:27
  39.2 0.9 sub.9
  40.1 15.5 %all_gather.6 = f32[2048,64]{0,1:T(8,128)S(1)} all-gather(f32[2048,16]{0,1:T(8,128)S(1)} %sub.9), channel_id=1, replica_groups=mesh['grp'=2,'row'=4,'col'=4] {'col'}, dimensions={1}, use_global_device_ids=true | all-gather | bytes 655360 | tf_op jit(solution)/shard_map/all_gather | solution.py:34
  55.6 5.5 %convolution_bitcast_fusion.3 = f32[512,64]{0,1:T(8,128)} fusion(f32[2048,64]{0,1:T(8,128)S(1)} %all_gather.6, f32[2048,512]{1,0:T(8,128)} %param.4), kind=kOutput, calls=%fused_computation.3 | convolution fusion | flops 805306368 | bytes 4849664 | tf_op jit(solution)/shard_map/dot_general | solution.py:10
  61.2 30.3 %all-reduce.7.cloned.1.call-done = f32[512,64]{0,1:T(8,128)} async-done(((f32[512,64]{0,1:T(8,128)}), f32[512,64]{0,1:T(8,128)}) %all-reduce.7.cloned.1.call-update) | async-done | bytes 131088 | tf_op jit(solution)/shard_map/psum | solution.py:35
  91.5 2.3 convolution_bitcast_fusion.7
  93.9 35.2 %all-reduce.9.cloned.1.call-done = f32[512,64]{0,1:T(8,128)} async-done(((f32[512,64]{0,1:T(8,128)}), f32[512,64]{0,1:T(8,128)}) %all-reduce.9.cloned.1.call-update) | async-done | bytes 131088 | tf_op jit(solution)/shard_map/psum | solution.py:35
  129.1 2.7 convolution_bitcast_fusion.6
  131.8 31.6 %all-reduce.11.cloned.1.call-done = f32[512,64]{0,1:T(8,128)} async-done(((f32[512,64]{0,1:T(8,128)}), f32[512,64]{0,1:T(8,128)}) %all-reduce.11.cloned.1.call-update) | async-done | bytes 131088 | tf_op jit(solution)/shard_map/psum | solution.py:36
  163.4 0.9 add.27
  164.3 7.0 %convolution_bitcast_fusion.1 = f32[2048,64]{0,1:T(8,128)} fusion(f32[512,64]{0,1:T(8,128)S(1)} %add.27, f32[2048,512]{1,0:T(8,128)} %param.4), kind=kOutput, calls=%fused_computation.1 | convolution fusion | flops 805306368 | bytes 4849664 | tf_op jit(solution)/shard_map/dot_general | solution.py:20
  171.4 21.9 %reduce-scatter.6.cloned.1.call-done = f32[2048,16]{0,1:T(8,128)} async-done(((f32[2048,64]{0,1:T(8,128)}), f32[2048,16]{0,1:T(8,128)}) %reduce-scatter.6.cloned.1.call-update) | async-done | bytes 131088 | tf_op jit(solution)/shard_map/reduce_scatter | solution.py:27
  193.4 0.9 sub.10
  194.3 15.6 %all_gather.7 = f32[2048,64]{0,1:T(8,128)S(1)} all-gather(f32[2048,16]{0,1:T(8,128)S(1)} %sub.10), channel_id=1, replica_groups=mesh['grp'=2,'row'=4,'col'=4] {'col'}, dimensions={1}, use_global_device_ids=true | all-gather | bytes 655360 | tf_op jit(solution)/shard_map/all_gather | solution.py:34
  209.9 5.5 %convolution_bitcast_fusion.2 = f32[512,64]{0,1:T(8,128)} fusion(f32[2048,64]{0,1:T(8,128)S(1)} %all_gather.7, f32[2048,512]{1,0:T(8,128)} %param.4), kind=kOutput, calls=%fused_computation.2 | convolution fusion | flops 805306368 | bytes 4849664 | tf_op jit(solution)/shard_map/dot_general | solution.py:10
  215.5 30.2 %all-reduce.13.cloned.1.call-done = f32[512,64]{0,1:T(8,128)} async-done(((f32[512,64]{0,1:T(8,128)}), f32[512,64]{0,1:T(8,128)}) %all-reduce.13.cloned.1.call-update) | async-done | bytes 131088 | tf_op jit(solution)/shard_map/psum | solution.py:35
  245.7 2.3 convolution_bitcast_fusion.5
  248.1 35.2 %all-reduce.15.cloned.1.call-done = f32[512,64]{0,1:T(8,128)} async-done(((f32[512,64]{0,1:T(8,128)}), f32[512,64]{0,1:T(8,128)}) %all-reduce.15.cloned.1.call-update) | async-done | bytes 131088 | tf_op jit(solution)/shard_map/psum | solution.py:35
  283.3 2.7 convolution_bitcast_fusion.4
  286.1 31.6 %all-reduce.17.cloned.1.call-done = f32[512,64]{0,1:T(8,128)} async-done(((f32[512,64]{0,1:T(8,128)}), f32[512,64]{0,1:T(8,128)}) %all-reduce.17.cloned.1.call-update) | async-done | bytes 131088 | tf_op jit(solution)/shard_map/psum | solution.py:36
  317.7 7.1 %convolution_bitcast_fusion = f32[2048,64]{0,1:T(8,128)} fusion(f32[2048,512]{1,0:T(8,128)} %param.4, f32[512,64]{0,1:T(8,128)S(1)} %add.27, f32[512,64]{0,1:T(8,128)} %all-reduce.17.cloned.1.call-done), kind=kOutput, calls=%fused_computation | convolution fusion | flops 805339136 | bytes 4980736 | tf_op jit(solution)/shard_map/dot_general | solution.py:20
  325.6 21.3 %reduce-scatter.8.cloned.1.call-done = f32[2048,16]{0,1:T(8,128)} async-done(((f32[2048,64]{0,1:T(8,128)}), f32[2048,16]{0,1:T(8,128)}) %reduce-scatter.8.cloned.1.call-update) | async-done | bytes 131088 | tf_op jit(solution)/shard_map/reduce_scatter | solution.py:27
  346.9 1.6 sub.11
  (29 shorter events, 1.2 us)
Async XLA Ops:
  7.2 84.3 %copy-start = (f32[512,512]{1,0:T(8,128)S(1)}, f32[512,512]{1,0:T(8,128)}, u32[]{:S(2)}) copy-start(f32[512,512]{1,0:T(8,128)} %param.7) | copy-start | bytes 3145732
  7.2 32.0 %copy-start.1 = (f32[2048,16]{0,1:T(8,128)S(1)}, f32[2048,16]{0,1:T(8,128)}, u32[]{:S(2)}) copy-start(f32[2048,16]{0,1:T(8,128)} %param.5) | copy-start | bytes 393220
  7.2 32.0 %reduce-scatter.4.cloned.1.call-start = ((), (), s32[]{:S(2)}) async-start(), calls=%async_computation.3 | async-start | bytes 655360 | tf_op jit(solution)/shard_map/reduce_scatter | solution.py:27
  14.5 77.0 %all-reduce.7.cloned.1.call-start = ((), (), s32[]{:S(2)}) async-start(), calls=%async_computation.4 | async-start | bytes 262144 | tf_op jit(solution)/shard_map/psum | solution.py:35
  40.1 123.3 %copy-start.2 = (f32[512,64]{0,1:T(8,128)S(1)}, f32[512,64]{0,1:T(8,128)}, u32[]{:S(2)}) copy-start(f32[512,64]{0,1:T(8,128)} %param.6) | copy-start | bytes 393220
  61.1 67.9 %all-reduce.9.cloned.1.call-start = ((), (), s32[]{:S(2)}) async-start(), calls=%async_computation.5 | async-start | bytes 262144 | tf_op jit(solution)/shard_map/psum | solution.py:35
  93.8 69.6 %all-reduce.11.cloned.1.call-start = ((), (), s32[]{:S(2)}) async-start(), calls=%async_computation.6 | async-start | bytes 262144 | tf_op jit(solution)/shard_map/psum | solution.py:36
  131.8 61.6 %reduce-scatter.6.cloned.1.call-start = ((), (), s32[]{:S(2)}) async-start(), calls=%async_computation.7 | async-start | bytes 655360 | tf_op jit(solution)/shard_map/reduce_scatter | solution.py:27
  171.4 74.3 %all-reduce.13.cloned.1.call-start = ((), (), s32[]{:S(2)}) async-start(), calls=%async_computation.8 | async-start | bytes 262144 | tf_op jit(solution)/shard_map/psum | solution.py:35
  215.5 109.4 %copy-start.3 = (f32[512,64]{0,1:T(8,128)S(1)}, f32[512,64]{0,1:T(8,128)}, u32[]{:S(2)}) copy-start(f32[512,64]{0,1:T(8,128)} %all-reduce.11.cloned.1.call-done) | copy-start | bytes 393220
  215.5 67.8 %all-reduce.15.cloned.1.call-start = ((), (), s32[]{:S(2)}) async-start(), calls=%async_computation.9 | async-start | bytes 262144 | tf_op jit(solution)/shard_map/psum | solution.py:35
  248.1 69.6 %all-reduce.17.cloned.1.call-start = ((), (), s32[]{:S(2)}) async-start(), calls=%async_computation.10 | async-start | bytes 262144 | tf_op jit(solution)/shard_map/psum | solution.py:36
  286.0 60.8 %reduce-scatter.8.cloned.1.call-start = ((), (), s32[]{:S(2)}) async-start(), calls=%async_computation.11 | async-start | bytes 655360 | tf_op jit(solution)/shard_map/reduce_scatter | solution.py:27
  317.7 7.2 %copy-start.4 = (f32[512,64]{0,1:T(8,128)S(1)}, f32[512,64]{0,1:T(8,128)}, u32[]{:S(2)}) copy-start(f32[512,64]{0,1:T(8,128)} %all-reduce.17.cloned.1.call-done) | copy-start | bytes 393220
Sparse Core Ops, SparseCore 0:
  14.6 24.5 reduce-scatter.3
  61.3 30.1 all-reduce.6
  94.4 34.6 all-reduce.8
  131.9 31.4 all-reduce.10
  171.5 21.8 reduce-scatter.5
  215.6 30.1 all-reduce.12
  248.6 34.6 all-reduce.14
  286.2 31.4 all-reduce.16
  325.0 21.8 reduce-scatter.7
where the time goes:
time: 355 us
  waiting for transfers between devices  262 us (74%)
  matrix products  42.4 us (12%)
  blocking collectives  31.1 us (9%)
  between operations  13.9 us (4%)
  other arithmetic  5.01 us (1%)
    psum x2, waiting for transfers between devices, local(): lax.psum(transposed_product(inverse_factor, lax.psum(partial_value, 'row'...  70.4 us
    reduce_scatter x3, waiting for transfers between devices, residual_parts(): lax.psum_scatter(fitted, 'col', scatter_dimension=1, tiled=True)  67.9 us
    psum x2, waiting for transfers between devices, local(): change = lax.psum(plain_product(inverse_factor, inner), 'row')  63.2 us
    psum x2, waiting for transfers between devices, local(): lax.psum(partial_value, 'row')  60.5 us
    all_gather x2, blocking collectives, local(): lax.all_gather(own, 'col', axis=1, tiled=True)  31.1 us
    dot_general x5, matrix products, plain_product(): jnp.dot(left, right, precision=lax.Precision.HIGHEST, preferred_element_t...  26.7 us
    dot_general x4, matrix products, transposed_product(): lax.dot_general(left, right, (((0,), (0,)), ((), ())), precision=lax.Prec...  15.6 us
  transfers between devices with their start and end apart: 9, of which 9 were waited for; matrix products, arithmetic and copies ran while one was open for 0% of the time, Pallas kernels for 0%

commit v1 on v0

--- a/solution.py
+++ b/solution.py
@@ -32,7 +32,8 @@
     for step in range(ITERS):
         own, whole = residual_parts(field)
         partial_value = transposed_product(dosage, lax.all_gather(own, "col", axis=1, tiled=True))
-        inner = lax.psum(transposed_product(inverse_factor, lax.psum(partial_value, "row")), "col")
+        raw = transposed_product(inverse_factor, lax.psum(partial_value, "row"))
+        inner = jnp.sum(lax.all_gather(raw, "col"), axis=0)
         change = lax.psum(plain_product(inverse_factor, inner), "row")
         field = field + change
         total = total + change

time: 355 us -> 315 us (0.89)
  waiting for transfers between devices: 262 us -> 194 us
  blocking collectives: 31.1 us -> 60.4 us
    psum x4 -> x2, waiting for transfers between devices: 131 us -> 60.5 us  [local(): raw = transposed_product(inverse_factor, lax.psum(partial_value, 'row'))]
    all_gather x0 -> x2, blocking collectives: none -> 29.4 us  [local(): inner = jnp.sum(lax.all_gather(raw, 'col'), axis=0)]
  transfers between devices with their start and end apart: 9 -> 7, of which waited for: 9 -> 7; matrix products, arithmetic and copies ran while one was open for 0% -> 0% of each run, Pallas kernels for 0% -> 0%
where the time goes in v1:
time: 315 us
  waiting for transfers between devices  194 us (62%)
  blocking collectives  60.4 us (19%)
  matrix products  39.3 us (12%)
  between operations  14.2 us (5%)
  other arithmetic  5.62 us (2%)
    reduce_scatter x3, waiting for transfers between devices, residual_parts(): lax.psum_scatter(fitted, 'col', scatter_dimension=1, tiled=True)  67.9 us
    psum x2, waiting for transfers between devices, local(): change = lax.psum(plain_product(inverse_factor, inner), 'row')  65.7 us
    psum x2, waiting for transfers between devices, local(): raw = transposed_product(inverse_factor, lax.psum(partial_value, 'row'))  60.5 us
    all_gather x2, blocking collectives, local(): lax.all_gather(own, 'col', axis=1, tiled=True)  31 us
    all_gather x2, blocking collectives, local(): inner = jnp.sum(lax.all_gather(raw, 'col'), axis=0)  29.4 us
    dot_general x5, matrix products, plain_product(): jnp.dot(left, right, precision=lax.Precision.HIGHEST, preferred_element_t...  24.9 us
    dot_general x4, matrix products, transposed_product(): lax.dot_general(left, right, (((0,), (0,)), ((), ())), precision=lax.Prec...  14.3 us
  transfers between devices with their start and end apart: 7, of which 7 were waited for; matrix products, arithmetic and copies ran while one was open for 0% of the time, Pallas kernels for 0%

profile of v1, /device:TPU:0, one launch (start us, length us, event | category | flops | bytes accessed | tf_op | source)
XLA Modules:
  0.0 314.8 jit_solution(4018952855517623273)
XLA Ops:
  7.2 7.2 %fusion.1 = f32[2048,64]{0,1:T(8,128)} fusion(f32[2048,512]{1,0:T(8,128)} %param.4, f32[512,64]{0,1:T(8,128)} %param.6), kind=kOutput, calls=%fused_computation.9 | convolution fusion | flops 805306368 | bytes 4849664 | tf_op jit(solution)/shard_map/dot_general | solution.py:20
  14.5 24.7 %reduce-scatter.4.cloned.1.call-done = f32[2048,16]{0,1:T(8,128)} async-done(((f32[2048,64]{0,1:T(8,128)}), f32[2048,16]{0,1:T(8,128)}) %reduce-scatter.4.cloned.1.call-update) | async-done | bytes 131088 | tf_op jit(solution)/shard_map/reduce_scatter | solution.py:27
  39.2 0.9 sub.9
  40.1 15.3 %all_gather.18 = f32[2048,64]{0,1:T(8,128)S(1)} all-gather(f32[2048,16]{0,1:T(8,128)S(1)} %sub.9), channel_id=1, replica_groups=mesh['grp'=2,'row'=4,'col'=4] {'col'}, dimensions={1}, use_global_device_ids=true | all-gather | bytes 655360 | tf_op jit(solution)/shard_map/all_gather | solution.py:34
  55.5 5.5 %convolution_bitcast_fusion.3 = f32[512,64]{0,1:T(8,128)} fusion(f32[2048,64]{0,1:T(8,128)S(1)} %all_gather.18, f32[2048,512]{1,0:T(8,128)} %param.4), kind=kOutput, calls=%fused_computation.3 | convolution fusion | flops 805306368 | bytes 4849664 | tf_op jit(solution)/shard_map/dot_general | solution.py:10
  61.1 30.3 %all-reduce.5.cloned.1.call-done = f32[512,64]{0,1:T(8,128)} async-done(((f32[512,64]{0,1:T(8,128)}), f32[512,64]{0,1:T(8,128)}) %all-reduce.5.cloned.1.call-update) | async-done | bytes 131088 | tf_op jit(solution)/shard_map/psum | solution.py:35
  91.4 1.7 convolution_bitcast_fusion.7
  93.1 14.7 %all-gather = f32[2048,64]{0,1:T(8,128)S(1)} all-gather(f32[512,64]{0,1:T(8,128)S(1)} %convolution_bitcast_fusion.7), channel_id=2, replica_groups=mesh['grp'=2,'row'=4,'col'=4] {'col'}, dimensions={0}, use_global_device_ids=true | all-gather | bytes 655360 | tf_op jit(solution)/shard_map/all_gather | solution.py:36
  108.4 1.8 convolution_bitcast_fusion.6
  110.3 32.8 %all-reduce.7.cloned.1.call-done = f32[512,64]{0,1:T(8,128)} async-done(((f32[512,64]{0,1:T(8,128)}), f32[512,64]{0,1:T(8,128)}) %all-reduce.7.cloned.1.call-update) | async-done | bytes 131088 | tf_op jit(solution)/shard_map/psum | solution.py:37
  143.1 0.9 add.23
  144.1 7.0 %convolution_bitcast_fusion.1 = f32[2048,64]{0,1:T(8,128)} fusion(f32[512,64]{0,1:T(8,128)S(1)} %add.23, f32[2048,512]{1,0:T(8,128)} %param.4), kind=kOutput, calls=%fused_computation.1 | convolution fusion | flops 805306368 | bytes 4849664 | tf_op jit(solution)/shard_map/dot_general | solution.py:20
  151.2 22.0 %reduce-scatter.6.cloned.1.call-done = f32[2048,16]{0,1:T(8,128)} async-done(((f32[2048,64]{0,1:T(8,128)}), f32[2048,16]{0,1:T(8,128)}) %reduce-scatter.6.cloned.1.call-update) | async-done | bytes 131088 | tf_op jit(solution)/shard_map/reduce_scatter | solution.py:27
  173.1 0.9 sub.10
  174.1 15.6 %all_gather.21 = f32[2048,64]{0,1:T(8,128)S(1)} all-gather(f32[2048,16]{0,1:T(8,128)S(1)} %sub.10), channel_id=1, replica_groups=mesh['grp'=2,'row'=4,'col'=4] {'col'}, dimensions={1}, use_global_device_ids=true | all-gather | bytes 655360 | tf_op jit(solution)/shard_map/all_gather | solution.py:34
  189.7 5.5 %convolution_bitcast_fusion.2 = f32[512,64]{0,1:T(8,128)} fusion(f32[2048,64]{0,1:T(8,128)S(1)} %all_gather.21, f32[2048,512]{1,0:T(8,128)} %param.4), kind=kOutput, calls=%fused_computation.2 | convolution fusion | flops 805306368 | bytes 4849664 | tf_op jit(solution)/shard_map/dot_general | solution.py:10
  195.3 30.2 %all-reduce.9.cloned.1.call-done = f32[512,64]{0,1:T(8,128)} async-done(((f32[512,64]{0,1:T(8,128)}), f32[512,64]{0,1:T(8,128)}) %all-reduce.9.cloned.1.call-update) | async-done | bytes 131088 | tf_op jit(solution)/shard_map/psum | solution.py:35
  225.5 1.7 convolution_bitcast_fusion.5
  227.1 14.7 %all-gather.1 = f32[2048,64]{0,1:T(8,128)S(1)} all-gather(f32[512,64]{0,1:T(8,128)S(1)} %convolution_bitcast_fusion.5), channel_id=3, replica_groups=mesh['grp'=2,'row'=4,'col'=4] {'col'}, dimensions={0}, use_global_device_ids=true | all-gather | bytes 655360 | tf_op jit(solution)/shard_map/all_gather | solution.py:36
  242.5 1.8 convolution_bitcast_fusion.4
  244.4 32.8 %all-reduce.11.cloned.1.call-done = f32[512,64]{0,1:T(8,128)} async-done(((f32[512,64]{0,1:T(8,128)}), f32[512,64]{0,1:T(8,128)}) %all-reduce.11.cloned.1.call-update) | async-done | bytes 131088 | tf_op jit(solution)/shard_map/psum | solution.py:37
  277.2 7.1 %convolution_bitcast_fusion = f32[2048,64]{0,1:T(8,128)} fusion(f32[2048,512]{1,0:T(8,128)} %param.4, f32[512,64]{0,1:T(8,128)S(1)} %add.23, f32[512,64]{0,1:T(8,128)} %all-reduce.11.cloned.1.call-done), kind=kOutput, calls=%fused_computation | convolution fusion | flops 805339136 | bytes 4980736 | tf_op jit(solution)/shard_map/dot_general | solution.py:20
  285.1 21.3 %reduce-scatter.8.cloned.1.call-done = f32[2048,16]{0,1:T(8,128)} async-done(((f32[2048,64]{0,1:T(8,128)}), f32[2048,16]{0,1:T(8,128)}) %reduce-scatter.8.cloned.1.call-update) | async-done | bytes 131088 | tf_op jit(solution)/shard_map/reduce_scatter | solution.py:27
  306.4 1.6 sub.11
  (29 shorter events, 2.4 us)
Async XLA Ops:
  7.2 84.2 %copy-start = (f32[512,512]{1,0:T(8,128)S(1)}, f32[512,512]{1,0:T(8,128)}, u32[]{:S(2)}) copy-start(f32[512,512]{1,0:T(8,128)} %param.7) | copy-start | bytes 3145732
  7.2 32.0 %copy-start.1 = (f32[2048,16]{0,1:T(8,128)S(1)}, f32[2048,16]{0,1:T(8,128)}, u32[]{:S(2)}) copy-start(f32[2048,16]{0,1:T(8,128)} %param.5) | copy-start | bytes 393220
  7.2 32.0 %reduce-scatter.4.cloned.1.call-start = ((), (), s32[]{:S(2)}) async-start(), calls=%async_computation.3 | async-start | bytes 655360 | tf_op jit(solution)/shard_map/reduce_scatter | solution.py:27
  14.5 76.9 %all-reduce.5.cloned.1.call-start = ((), (), s32[]{:S(2)}) async-start(), calls=%async_computation.4 | async-start | bytes 262144 | tf_op jit(solution)/shard_map/psum | solution.py:35
  55.5 87.7 %copy-start.2 = (f32[512,64]{0,1:T(8,128)S(1)}, f32[512,64]{0,1:T(8,128)}, u32[]{:S(2)}) copy-start(f32[512,64]{0,1:T(8,128)} %param.6) | copy-start | bytes 393220
  61.0 82.1 %all-reduce.7.cloned.1.call-start = ((), (), s32[]{:S(2)}) async-start(), calls=%async_computation.5 | async-start | bytes 262144 | tf_op jit(solution)/shard_map/psum | solution.py:37
  110.2 62.9 %reduce-scatter.6.cloned.1.call-start = ((), (), s32[]{:S(2)}) async-start(), calls=%async_computation.6 | async-start | bytes 655360 | tf_op jit(solution)/shard_map/reduce_scatter | solution.py:27
  151.1 74.3 %all-reduce.9.cloned.1.call-start = ((), (), s32[]{:S(2)}) async-start(), calls=%async_computation.7 | async-start | bytes 262144 | tf_op jit(solution)/shard_map/psum | solution.py:35
  195.2 82.0 %all-reduce.11.cloned.1.call-start = ((), (), s32[]{:S(2)}) async-start(), calls=%async_computation.8 | async-start | bytes 262144 | tf_op jit(solution)/shard_map/psum | solution.py:37
  241.8 42.5 %copy-start.3 = (f32[512,64]{0,1:T(8,128)S(1)}, f32[512,64]{0,1:T(8,128)}, u32[]{:S(2)}) copy-start(f32[512,64]{0,1:T(8,128)} %all-reduce.7.cloned.1.call-done) | copy-start | bytes 393220
  244.3 62.1 %reduce-scatter.8.cloned.1.call-start = ((), (), s32[]{:S(2)}) async-start(), calls=%async_computation.9 | async-start | bytes 655360 | tf_op jit(solution)/shard_map/reduce_scatter | solution.py:27
  277.2 7.2 %copy-start.4 = (f32[512,64]{0,1:T(8,128)S(1)}, f32[512,64]{0,1:T(8,128)}, u32[]{:S(2)}) copy-start(f32[512,64]{0,1:T(8,128)} %all-reduce.11.cloned.1.call-done) | copy-start | bytes 393220
Sparse Core Ops, SparseCore 0:
  14.6 24.5 reduce-scatter.3
  61.2 30.1 all-reduce.4
  110.4 32.7 all-reduce.6
  151.3 21.8 reduce-scatter.5
  195.3 30.0 all-reduce.8
  244.4 32.7 all-reduce.10
  284.5 21.8 reduce-scatter.7
